TPU v7x, 32 devices: a whole 2x2x4 slice. The times are simulated.
32 devices in a mesh: rows: 8 (over z, y), vecs: 4 (over x, core).
Axes of the slice: x: 2, y: 2, z: 4, core: 2. Of those that a mesh axis runs over, the one named last changes fastest.
Arguments:
- vectors: bfloat16 [24576, 512], P('rows', 'vecs'), may hold values from -8 to 8
- node_mass: float32 [24576], P('rows'), may hold values from 0.5 to 2
- cable_stiff: float32 [24576], P('rows'), may hold values from 0.1 to 1
- cable_nodes: int32 [8, 4], P('rows'), may hold values from 1 to 1152, 2304 in all within a row
- deck_rigidity: float32 [], replicated, may hold values from 0.3 to 1
- anchor_rows: int32 [8, 8, 4], P('rows'), may hold values from 0 to 3072, as said below
- anchor_stiff: float32 [8, 8, 4], P('rows'), may hold values from 0.2 to 1, as said below
- cut_low: float32 [], replicated, may hold values from 1.5 to 2.5
- top_bound: float32 [], replicated, may hold values from 7 to 9
Outputs:
- basis: bfloat16 [24576, 512], P('rows', 'vecs')
Inputs may be any that keep to these rules, and one draw needn't show every extreme that they name: anchor_rows[r, q, s] is a node of partition r coupled through slot s to partition q, or 3072 where the slot is empty; slot s of r towards q is live exactly when slot s of q towards r is; live slots come first; no partition has live slots towards itself; a partition that is not a pylon partition has live slots only towards the partitions beside it in the cyclic order, which fill all 4 slots, and towards at most 4 pylon partitions; pylon partitions come in pairs half the cyclic order apart, and the two of a pair fill all 4 slots towards each other. anchor_stiff[r, q, s] equals anchor_stiff[q, r, s].
All inputs are finite; a program needn't handle non-finite values.
Results may differ from a plain program's by a relative error of at most 0.0072.
The roundings to bfloat16 on the way count: a program that leaves them out, or rounds other values in their place, can miss the bound.
Values may be sent and summed in bfloat16 or wider, within the bound.
A program may use at most 64 MiB of HBM per device.

v0:
```python
import functools

import jax
import jax.numpy as jnp
from jax import lax
from jax.experimental import pallas as pl
from jax.experimental.pallas import tpu as pltpu
from jax.sharding import PartitionSpec as P

CABLE_ROWS = 2304
MESH = pl.DeviceIdType.MESH
PAD = 8


NB = 128
HI = lax.Precision.HIGHEST


def spread(tile, lane):
    return jnp.broadcast_to(tile[:, lane : lane + 1], tile.shape)


def eliminate(block):
    lane = lax.broadcasted_iota(jnp.int32, (8, NB), 1)
    sub = lax.broadcasted_iota(jnp.int32, (8, NB), 0)
    tiles = NB // 8
    left = [block[8 * t : 8 * t + 8, :] for t in range(tiles)]
    right = [jnp.where(lane == sub + 8 * t, 1.0, 0.0).astype(jnp.float32) for t in range(tiles)]
    for g in range(tiles):
        home, away = left[g], right[g]
        column = [spread(home, 8 * g + i) for i in range(8)]
        scales, rows = [], []
        for i in range(8):
            scale = lax.rsqrt(column[i][i : i + 1, :])
            scales.append(scale)
            column[i] = column[i] * scale
            rows.append([column[i][n : n + 1, :] for n in range(8)])
            for n in range(i + 1, 8):
                column[n] = column[n] - column[i] * rows[i][n]
        for i in range(8):
            upper = home[i : i + 1, :] * scales[i]
            inverse = away[i : i + 1, :] * scales[i]
            home = jnp.where(sub > i, home - column[i] * upper, jnp.where(sub == i, upper, home))
            away = jnp.where(sub > i, away - column[i] * inverse, jnp.where(sub == i, inverse, away))
        right[g] = away
        for t in range(g + 1, tiles):
            factor = [spread(left[t], 8 * g + i) for i in range(8)]
            for i in range(8):
                factor[i] = factor[i] * scales[i]
                for n in range(i + 1, 8):
                    factor[n] = factor[n] - factor[i] * rows[i][n]
            for i in range(8):
                left[t] = left[t] - factor[i] * home[i : i + 1, :]
                right[t] = right[t] - factor[i] * away[i : i + 1, :]
    return jnp.concatenate(right, axis=0)


def mm(a, b, dims):
    return lax.dot_general(a, b, (dims, ((), ())), precision=HI, preferred_element_type=jnp.float32)


def inverse_factor(gram_ref, inv_ref, between):
    size = gram_ref.shape[0]
    inv_ref[...] = jnp.zeros_like(inv_ref)
    for k in range(size // NB):
        lo, hi = k * NB, (k + 1) * NB
        diag_inv = eliminate(gram_ref[lo:hi, lo:hi])
        if k == (size // NB - 1) // 2:
            between()
        if k:
            inv_ref[lo:hi, :lo] = mm(diag_inv, inv_ref[lo:hi, :lo], ((1,), (0,)))
        inv_ref[lo:hi, lo:hi] = diag_inv
        if hi < size:
            panel = mm(gram_ref[hi:, lo:hi], diag_inv, ((1,), (1,)))
            for i in range(hi, size, NB):
                part = panel[i - hi : i - hi + NB]
                gram_ref[i : i + NB, hi : i + NB] -= mm(part, panel[: i - hi + NB], ((1,), (1,)))
            inv_ref[hi:, :hi] -= mm(panel, inv_ref[lo:hi, :hi], ((1,), (0,)))


def travel_plan(splits):
    if splits != 4:
        direct = [
            (block, target, block, piece)
            for target in range(splits)
            for block in range(target)
            for piece in range(splits)
            if piece != target
        ]
        return direct, []
    first = [(0, 2, 0, 0), (0, 3, 0, 1), (1, 2, 1, 0), (1, 3, 1, 1)]
    first += [(2, 3, 0, 2), (2, 3, 1, 2), (3, 2, 0, 3), (3, 2, 1, 3)]
    first += [(0, 1, 0, 0), (0, 1, 0, 2), (0, 1, 0, 3), (2, 3, 2, 0), (2, 3, 2, 1), (2, 3, 2, 2)]
    second = [(2, 3, 0, 0), (2, 3, 1, 0), (3, 2, 0, 1), (3, 2, 1, 1)]
    return first, second


def split_three(value):
    high = value.astype(jnp.bfloat16)
    rest = value - high.astype(jnp.float32)
    middle = rest.astype(jnp.bfloat16)
    low = (rest - middle.astype(jnp.float32)).astype(jnp.bfloat16)
    return jnp.concatenate([high, middle, low], axis=0)


def kernel(
    parts,
    splits,
    x_ref,
    mass_ref,
    stiff_ref,
    nodes_ref,
    rigid_ref,
    rows_ref,
    spring_ref,
    low_ref,
    top_ref,
    out_ref,
    value_ref,
    first_ref,
    link_ref,
    diag_ref,
    hot_ref,
    force_ref,
    send_buf,
    recv_buf,
    cols_ref,
    sum_ref,
    half_ref,
    piece_ref,
    all_ref,
    gram_ref,
    inv_ref,
    ex_send,
    ex_recv,
    quarter_send,
    quarter_recv,
    travel_send,
    travel_recv,
    fold_send,
    fold_recv,
    piece_send,
    piece_recv,
    give_send,
    give_recv,
    grow_send,
    grow_recv,
    relay_send,
    relay_recv,
):
    me = lax.axis_index("rows")
    col = lax.axis_index("vecs")
    count, width = x_ref.shape
    slots = rows_ref.shape[2]
    total_rows = count * parts

    barrier = pltpu.get_barrier_semaphore()
    for k in range(1, splits):
        pl.semaphore_signal(
            barrier, inc=1, device_id=(me, lax.rem(col + k, splits)), device_id_type=MESH
        )

    def greet(k, carry):
        pl.semaphore_signal(
            barrier, inc=1, device_id=(lax.rem(me + k, parts), col), device_id_type=MESH
        )
        return carry

    lax.fori_loop(1, parts, greet, 0)
    pl.semaphore_wait(barrier, parts - 1 + splits - 1)

    top = jnp.full((1, width), top_ref[0], jnp.float32)
    bottom = jnp.full((1, width), low_ref[0], jnp.float32)
    center = (top + bottom) * 0.5
    inverse_half = 1.0 / ((top - bottom) * 0.5)

    chunk = count // splits
    zero_pad = jnp.zeros((PAD, width), jnp.float32)
    for ref in (value_ref, first_ref, link_ref):
        ref[0:PAD, :] = zero_pad
        ref[PAD + count :, :] = zero_pad
    for lo in range(0, count, chunk):
        value_ref[PAD + lo : PAD + lo + chunk, :] = x_ref[lo : lo + chunk, :].astype(jnp.float32)

    def remote(turn, k, target):
        return pltpu.make_async_remote_copy(
            src_ref=send_buf.at[turn, target],
            dst_ref=recv_buf.at[turn, me],
            send_sem=ex_send.at[turn, k],
            recv_sem=ex_recv.at[turn, k],
            device_id=(target, col),
            device_id_type=MESH,
        )

    def arrival(turn, k):
        source = lax.rem(me + parts - k, parts)
        return pltpu.make_async_remote_copy(
            src_ref=send_buf.at[turn, source],
            dst_ref=recv_buf.at[turn, source],
            send_sem=ex_send.at[turn, k],
            recv_sem=ex_recv.at[turn, k],
            device_id=(source, col),
            device_id_type=MESH,
        )

    unroll = parts <= 8

    def send_anchors(turn, ref):
        first_row = ref[PAD + CABLE_ROWS : PAD + CABLE_ROWS + 1, :]
        last_row = ref[PAD + count - 1 : PAD + count, :]
        blank = jnp.zeros((8 - slots - 2, width), jnp.float32)

        def pick(q, carry):
            picked = [
                ref[pl.ds(PAD + jnp.minimum(rows_ref[0, q, s], count - 1), 1), :] for s in range(slots)
            ]
            send_buf[turn, q] = jnp.concatenate(picked + [first_row, last_row, blank], axis=0)
            return carry

        lax.fori_loop(0, parts, pick, 0, unroll=unroll)

        def push(k, carry):
            remote(turn, k, lax.rem(me + k, parts)).start()
            return carry

        lax.fori_loop(1, parts, push, 0, unroll=unroll)
        recv_buf[turn, me] = send_buf[turn, me]

    def collect(turn, scale):
        def take(k, carry):
            arrival(turn, k).wait_recv()
            return carry

        lax.fori_loop(1, parts, take, 0, unroll=unroll)

        def pull(q, carry):
            difference = send_buf[turn, q] - recv_buf[turn, q]
            for s in range(slots):
                live = jnp.where(rows_ref[0, q, s] < count, spring_ref[0, q, s], 0.0)
                force_ref[pl.ds(q * slots + s, 1), :] = live * difference[s : s + 1, :]
            return carry

        lax.fori_loop(0, parts, pull, 0, unroll=unroll)
        before = recv_buf[turn, lax.rem(me + parts - 1, parts)]
        after = recv_buf[turn, lax.rem(me + 1, parts)]
        own = send_buf[turn, me]
        left_open = jnp.where(me > 0, rigid_ref[0], 0.0)
        right_open = jnp.where(me < parts - 1, rigid_ref[0], 0.0)
        edge = jnp.concatenate(
            [
                left_open * (own[slots : slots + 1] - before[slots + 1 : slots + 2]),
                right_open * (own[slots + 1 : slots + 2] - after[slots : slots + 1]),
                jnp.zeros((6, width), jnp.float32),
            ],
            axis=0,
        )
        force_ref[parts * slots : parts * slots + 8, :] = edge
        return split_three(force_ref[...] * scale)

    send_anchors(0, value_ref)

    forces = force_ref.shape[0]
    order = lax.rem(lax.broadcasted_iota(jnp.int32, (1, 3 * forces), 1), forces)
    ends = parts * slots
    target = jnp.where(order == ends, CABLE_ROWS, jnp.where(order == ends + 1, count - 1, count))

    def place_anchor(q, carry):
        for s in range(slots):
            carry = jnp.where(order == q * slots + s, rows_ref[0, q, s], carry)
        return carry

    target = lax.fori_loop(0, parts, place_anchor, target, unroll=unroll)

    lane = lax.broadcasted_iota(jnp.int32, (1, width), 1)
    rigid = rigid_ref[0]
    cuts = []
    running = nodes_ref[0, 0]
    for j in range(1, nodes_ref.shape[1]):
        cuts.append(running)
        running = running + nodes_ref[0, j]
    cuts.append(running)
    for r in range(count // width):
        place = lane + r * width
        open_link = place < CABLE_ROWS - 1
        for cut in cuts:
            open_link = open_link & (place + 1 != cut)
        deck_link = (place >= CABLE_ROWS) & (place < count - 1)
        link = jnp.where(open_link, stiff_ref[r : r + 1, :], jnp.where(deck_link, rigid, 0.0))
        lo = PAD + r * width
        link_ref[lo : lo + width, :] = jnp.broadcast_to(link, (width, width)).T
        mass = mass_ref[r : r + 1, :] - center
        diag_ref[r * width : (r + 1) * width, :] = jnp.broadcast_to(mass, (width, width)).T

    def base(ref, lo):
        at = PAD + lo
        here = ref[at : at + chunk, :]
        down = link_ref[at : at + chunk, :] * (here - ref[at + 1 : at + chunk + 1, :])
        up = link_ref[at - 1 : at + chunk - 1, :] * (here - ref[at - 1 : at + chunk - 1, :])
        return diag_ref[lo : lo + chunk, :] * here + down + up

    for lo in range(0, count, chunk):
        first_ref[PAD + lo : PAD + lo + chunk, :] = base(value_ref, lo) * inverse_half
        node = lax.broadcasted_iota(jnp.int32, (chunk, 3 * forces), 0) + lo
        hot_ref[lo : lo + chunk, :] = jnp.where(node == target, 1.0, 0.0).astype(jnp.bfloat16)

    pulls = collect(0, inverse_half)
    for lo in range(0, count, chunk):
        first_ref[PAD + lo : PAD + lo + chunk, :] += jnp.dot(
            hot_ref[lo : lo + chunk, :], pulls, preferred_element_type=jnp.float32
        )
    send_anchors(1, first_ref)
    double = 2.0 * inverse_half
    for lo in range(0, count, chunk):
        diag_ref[lo : lo + chunk, :] = (
            base(first_ref, lo) * double - value_ref[PAD + lo : PAD + lo + chunk, :]
        )
    pulls = collect(1, double)
    for lo in range(0, count, chunk):
        cols_ref[col, lo : lo + chunk, :] = (
            diag_ref[lo : lo + chunk, :]
            + jnp.dot(hot_ref[lo : lo + chunk, :], pulls, preferred_element_type=jnp.float32)
        ).astype(jnp.bfloat16)

    def share(owner, target, piece, k):
        rows = pl.ds(pl.multiple_of(piece * chunk, chunk), chunk)
        return pltpu.make_async_remote_copy(
            src_ref=cols_ref.at[owner, rows],
            dst_ref=cols_ref.at[owner, rows],
            send_sem=quarter_send.at[k],
            recv_sem=quarter_recv.at[k],
            device_id=(me, target),
            device_id_type=MESH,
        )

    for k in range(1, splits):
        target = lax.rem(col + k, splits)
        share(col, target, target, k).start()
    for k in range(1, splits):
        share(lax.rem(col + splits - k, splits), col, col, k).wait_recv()

    mine = pl.ds(pl.multiple_of(col * chunk, chunk), chunk)
    packed = jnp.concatenate([cols_ref[b, mine, :] for b in range(splits)], axis=1)
    for i in range(splits):
        rows = lax.dot_general(
            packed[:, i * width : (i + 1) * width],
            packed[:, : (i + 1) * width],
            (((0,), (0,)), ((), ())),
            preferred_element_type=jnp.float32,
        )
        for j in range(i + 1):
            at = (i * (i + 1) // 2 + j) * width
            sum_ref[at : at + width, :] = rows[:, j * width : (j + 1) * width]
    length = sum_ref.shape[0]
    used = splits * (splits + 1) // 2 * width
    if used < length:
        sum_ref[used:, :] = jnp.zeros((length - used, width), jnp.float32)

    bits = splits.bit_length() - 1
    start = 0
    offset = 0
    for b in range(bits):
        half = length >> (b + 1)
        bit = lax.rem(col // (1 << b), 2)
        partner = col + (1 << b) * (1 - 2 * bit)
        landing = half_ref.at[pl.ds(offset, half)]
        copy = pltpu.make_async_remote_copy(
            src_ref=sum_ref.at[pl.ds(pl.multiple_of(start + (1 - bit) * half, 8), half)],
            dst_ref=landing,
            send_sem=fold_send.at[b],
            recv_sem=fold_recv.at[b],
            device_id=(me, partner),
            device_id_type=MESH,
        )
        copy.start()
        copy.wait()
        start = pl.multiple_of(start + bit * half, 8)
        sum_ref[pl.ds(start, half), :] += half_ref[offset : offset + half, :]
        offset += half
    part = length // splits
    unit = part // parts

    def piece(q):
        return pl.ds(pl.multiple_of(start + q * unit, 8), unit)

    def send_piece(k, carry):
        target = lax.rem(me + k, parts)
        pltpu.make_async_remote_copy(
            src_ref=sum_ref.at[piece(target)],
            dst_ref=piece_ref.at[me],
            send_sem=piece_send.at[k],
            recv_sem=piece_recv.at[k],
            device_id=(target, col),
            device_id_type=MESH,
        ).start()
        return carry

    def piece_copy(k):
        source = lax.rem(me + parts - k, parts)
        return pltpu.make_async_remote_copy(
            src_ref=sum_ref.at[piece(source)],
            dst_ref=piece_ref.at[source],
            send_sem=piece_send.at[k],
            recv_sem=piece_recv.at[k],
            device_id=(source, col),
            device_id_type=MESH,
        )

    lax.fori_loop(1, parts, send_piece, 0, unroll=unroll)

    def add_piece(k, total):
        piece_copy(k).wait_recv()
        return total + piece_ref[lax.rem(me + parts - k, parts)]

    all_ref[piece(me), :] = lax.fori_loop(1, parts, add_piece, sum_ref[piece(me), :], unroll=unroll)

    def give(owner, target, k):
        return pltpu.make_async_remote_copy(
            src_ref=all_ref.at[piece(owner)],
            dst_ref=all_ref.at[piece(owner)],
            send_sem=give_send.at[k],
            recv_sem=give_recv.at[k],
            device_id=(target, col),
            device_id_type=MESH,
        )

    def give_start(k, carry):
        give(me, lax.rem(me + k, parts), k).start()
        return carry

    def give_wait(k, carry):
        give(lax.rem(me + parts - k, parts), me, k).wait_recv()
        return carry

    lax.fori_loop(1, parts, give_start, 0, unroll=unroll)
    last_bit = lax.rem(col // (splits // 2), 2)
    last_partner = col + (splits // 2) * (1 - 2 * last_bit)
    across = start + (1 - 2 * last_bit) * part

    def relay(region, k):
        source = lax.rem(me + parts - k, parts)
        rows = pl.ds(pl.multiple_of(region + source * unit, 8), unit)
        return pltpu.make_async_remote_copy(
            src_ref=all_ref.at[rows],
            dst_ref=all_ref.at[rows],
            send_sem=relay_send.at[k],
            recv_sem=relay_recv.at[k],
            device_id=(me, last_partner),
            device_id_type=MESH,
        )

    relay(start, 0).start()

    def relay_start(k, carry):
        give_wait(k, carry)
        relay(start, k).start()
        return carry

    def relay_wait(k, carry):
        relay(across, k).wait_recv()
        return carry

    lax.fori_loop(1, parts, relay_start, 0, unroll=unroll)
    lax.fori_loop(0, parts, relay_wait, 0, unroll=unroll)

    def relay_end(k, carry):
        relay(across, k).wait_send()
        return carry

    start = start - last_bit * part
    grown = []
    held = 2 * part
    for b in reversed(range(bits - 1)):
        bit = lax.rem(col // (1 << b), 2)
        partner = col + (1 << b) * (1 - 2 * bit)

        def grow(at):
            rows = pl.ds(pl.multiple_of(at, 8), held)
            return pltpu.make_async_remote_copy(
                src_ref=all_ref.at[rows],
                dst_ref=all_ref.at[rows],
                send_sem=grow_send.at[b],
                recv_sem=grow_recv.at[b],
                device_id=(me, partner),
                device_id_type=MESH,
            )

        copy = grow(start)
        copy.start()
        grown.append(copy)
        grow(start + (1 - 2 * bit) * held).wait_recv()
        start = start - bit * held
        held = 2 * held

    first_trips, second_trips = travel_plan(splits)

    def trip(number):
        _, target, block, piece = (first_trips + second_trips)[number]
        rows = pl.ds(piece * chunk, chunk)
        return pltpu.make_async_remote_copy(
            src_ref=cols_ref.at[block, rows],
            dst_ref=cols_ref.at[block, rows],
            send_sem=travel_send.at[number],
            recv_sem=travel_recv.at[number],
            device_id=(me, target),
            device_id_type=MESH,
        )

    def each_trip(numbers, end, act):
        trips = first_trips + second_trips
        for device in range(splits):
            own = [n for n in numbers if trips[n][end] == device]
            if own:

                @pl.when(col == device)
                def _():
                    for n in own:
                        act(trip(n))

    early = range(len(first_trips))
    late = range(len(first_trips), len(first_trips) + len(second_trips))
    each_trip(early, 0, lambda copy: copy.start())

    def pass_on():
        each_trip(early, 1, lambda copy: copy.wait_recv())
        each_trip(late, 0, lambda copy: copy.start())

    for i in range(splits):
        for j in range(i + 1):
            at = (i * (i + 1) // 2 + j) * width
            gram_ref[i * width : (i + 1) * width, j * width : (j + 1) * width] = all_ref[
                at : at + width, :
            ] * (1.0 / total_rows)
    inverse_factor(gram_ref, inv_ref, pass_on)
    each_trip(late, 1, lambda copy: copy.wait_recv())

    for device in range(splits):

        @pl.when(col == device)
        def _():
            used_width = (device + 1) * width
            factor = inv_ref[device * width : used_width, :used_width].astype(jnp.bfloat16)
            for lo in range(0, count, chunk):
                block = jnp.concatenate(
                    [cols_ref[b, lo : lo + chunk, :] for b in range(device + 1)], axis=1
                )
                out_ref[lo : lo + chunk, :] = lax.dot_general(
                    block, factor, (((1,), (1,)), ((), ())), preferred_element_type=jnp.float32
                ).astype(jnp.bfloat16)

    for k in range(1, splits):
        target = lax.rem(col + k, splits)
        share(col, target, target, k).wait_send()
    each_trip(range(len(first_trips) + len(second_trips)), 0, lambda copy: copy.wait_send())
    for copy in grown:
        copy.wait_send()

    def settle(k, carry):
        target = lax.rem(me + k, parts)
        remote(0, k, target).wait_send()
        remote(1, k, target).wait_send()
        piece_copy(k).wait_send()
        give(me, target, k).wait_send()
        return carry

    lax.fori_loop(1, parts, settle, 0, unroll=unroll)
    lax.fori_loop(0, parts, relay_end, 0, unroll=unroll)


def body(
    parts,
    splits,
    vectors,
    node_mass,
    cable_stiff,
    cable_nodes,
    deck_rigidity,
    anchor_rows,
    anchor_stiff,
    cut_low,
    top_bound,
):
    count, width = vectors.shape
    slots = anchor_rows.shape[2]
    forces = parts * slots + 8
    trips = sum(len(trips) for trips in travel_plan(splits))
    size = splits * width
    blocks = splits * (splits + 1) // 2
    unit = -(-(blocks * width) // (splits * parts * 8)) * 8
    length = unit * parts * splits
    bits = splits.bit_length() - 1
    vmem = pl.BlockSpec(memory_space=pltpu.VMEM)
    smem = pl.BlockSpec(memory_space=pltpu.SMEM)
    sem = pltpu.SemaphoreType.DMA
    f32 = jnp.float32
    return pl.pallas_call(
        functools.partial(kernel, parts, splits),
        out_shape=jax.ShapeDtypeStruct((count, width), jnp.bfloat16),
        in_specs=[vmem, vmem, vmem, smem, smem, smem, smem, smem, smem],
        out_specs=vmem,
        scratch_shapes=[
            pltpu.VMEM((count + 2 * PAD, width), f32),
            pltpu.VMEM((count + 2 * PAD, width), f32),
            pltpu.VMEM((count + 2 * PAD, width), f32),
            pltpu.VMEM((count, width), f32),
            pltpu.VMEM((count, 3 * forces), jnp.bfloat16),
            pltpu.VMEM((forces, width), f32),
            pltpu.VMEM((2, parts, 8, width), f32),
            pltpu.VMEM((2, parts, 8, width), f32),
            pltpu.VMEM((splits, count, width), jnp.bfloat16),
            pltpu.VMEM((length, width), f32),
            pltpu.VMEM((length, width), f32),
            pltpu.VMEM((parts, unit, width), f32),
            pltpu.VMEM((length, width), f32),
            pltpu.VMEM((size, size), f32),
            pltpu.VMEM((size, size), f32),
            sem((2, parts)),
            sem((2, parts)),
            sem((splits,)),
            sem((splits,)),
            sem((trips,)),
            sem((trips,)),
            sem((bits,)),
            sem((bits,)),
            sem((parts,)),
            sem((parts,)),
            sem((parts,)),
            sem((parts,)),
            sem((bits,)),
            sem((bits,)),
            sem((parts,)),
            sem((parts,)),
        ],
        compiler_params=pltpu.CompilerParams(
            collective_id=0, has_side_effects=True, vmem_limit_bytes=60 * 1024 * 1024
        ),
    )(
        vectors,
        node_mass.reshape(-1, width),
        cable_stiff.reshape(-1, width),
        cable_nodes,
        deck_rigidity.reshape(1),
        anchor_rows,
        anchor_stiff,
        cut_low.reshape(1),
        top_bound.reshape(1),
    )


def solution(mesh):
    return jax.shard_map(
        functools.partial(body, mesh.shape["rows"], mesh.shape["vecs"]),
        mesh=mesh,
        in_specs=(
            P("rows", "vecs"),
            P("rows"),
            P("rows"),
            P("rows", None),
            P(),
            P("rows", None, None),
            P("rows", None, None),
            P(),
            P(),
        ),
        out_specs=P("rows", "vecs"),
        check_vma=False,
    )
```

profile of v0, /device:TPU:3, one launch (start us, length us, event | category | flops | bytes accessed | tf_op | source)
XLA Modules:
  0.0 73.5 jit_solution(15417834437949198523)
XLA Ops:
  1.9 0.0 copy-start
  2.0 0.7 copy-done
  2.6 0.0 copy-start.1
  2.6 0.7 copy.10.rows_ref
  3.3 0.0 copy-done.1
  3.3 0.7 copy.11.spring_ref
  4.0 67.4 %shard_map.91 = bf16[3072,128]{1,0:T(8,128)(2,1)} custom-call(bf16[3072,128]{1,0:T(8,128)(2,1)} %x_ref.1, f32[24,128]{1,0:T(8,128)} %bitcast.8, f32[24,128]{1,0:T(8,128)} %bitcast.9, s32[1,4]{1,0:T(1,128)} %nodes_ref.1, f32[1]{0:T(128)} %bitcast.5.rigid_ref, s32[1,8,4]{2,1,0:T(8,128)} %copy.10.rows_ref, f32[1,8,4]{2,1,0:T(8,128)} %copy.11.spring_ref, ...), custom_call_target="tpu_custom_call" | custom-call | tf_op jit(solution)/shard_map/pallas_call | solution.py:595
  71.4 2.1 %copy.16 = bf16[3072,128]{1,0:T(8,128)(2,1)} copy(bf16[3072,128]{1,0:T(8,128)(2,1)} %shard_map.91) | data formatting | bytes 1572864
Async XLA Ops:
  1.9 0.7 copy-start
  2.6 0.7 copy-start.1
where the time goes:
time: 73.7 us; the launch traced here: 73.5 us
  Pallas kernels  67.4 us (91%)
  local copies, waits for them, and re-layouts  4.09 us (6%)
  between operations  1.96 us (3%)
    pallas_call x1, Pallas kernels, body(): pl.pallas_call(functools.partial(kernel, parts, splits), out_shape=jax.Sh...  67.4 us
    unnamed x7, local copies, waits for them, and re-layouts  4.09 us

commit v1 on v0

v1 whole, which is shorter than its diff:
```python
import functools

import jax
import jax.numpy as jnp
from jax import lax
from jax.experimental import pallas as pl
from jax.experimental.pallas import tpu as pltpu
from jax.sharding import PartitionSpec as P

CABLE_ROWS = 2304
MESH = pl.DeviceIdType.MESH
PAD = 8


NB = 128
HI = lax.Precision.HIGHEST


def spread(tile, lane):
    return jnp.broadcast_to(tile[:, lane : lane + 1], tile.shape)


def eliminate(block):
    lane = lax.broadcasted_iota(jnp.int32, (8, NB), 1)
    sub = lax.broadcasted_iota(jnp.int32, (8, NB), 0)
    tiles = NB // 8
    left = [block[8 * t : 8 * t + 8, :] for t in range(tiles)]
    right = [jnp.where(lane == sub + 8 * t, 1.0, 0.0).astype(jnp.float32) for t in range(tiles)]
    for g in range(tiles):
        home, away = left[g], right[g]
        column = [spread(home, 8 * g + i) for i in range(8)]
        scales, rows = [], []
        for i in range(8):
            scale = lax.rsqrt(column[i][i : i + 1, :])
            scales.append(scale)
            column[i] = column[i] * scale
            rows.append([column[i][n : n + 1, :] for n in range(8)])
            for n in range(i + 1, 8):
                column[n] = column[n] - column[i] * rows[i][n]
        for i in range(8):
            upper = home[i : i + 1, :] * scales[i]
            inverse = away[i : i + 1, :] * scales[i]
            home = jnp.where(sub > i, home - column[i] * upper, jnp.where(sub == i, upper, home))
            away = jnp.where(sub > i, away - column[i] * inverse, jnp.where(sub == i, inverse, away))
        right[g] = away
        for t in range(g + 1, tiles):
            factor = [spread(left[t], 8 * g + i) for i in range(8)]
            for i in range(8):
                factor[i] = factor[i] * scales[i]
                for n in range(i + 1, 8):
                    factor[n] = factor[n] - factor[i] * rows[i][n]
            for i in range(8):
                left[t] = left[t] - factor[i] * home[i : i + 1, :]
                right[t] = right[t] - factor[i] * away[i : i + 1, :]
    return jnp.concatenate(right, axis=0)


def mm(a, b, dims):
    return lax.dot_general(a, b, (dims, ((), ())), precision=HI, preferred_element_type=jnp.float32)


GROUPS = {
    "a": ((0, 0),),
    "b": ((1, 0), (1, 1)),
    "c": ((2, 0), (2, 1)),
    "d": ((2, 2), (3, 2), (3, 3)),
    "e": ((3, 0), (3, 1)),
}
OWNER = {"a": 3, "b": 2, "c": 2, "d": 2, "e": 2}
FOLDS = (("a", 0), ("b", 1), ("d", 2), ("c", 1), ("c", 2), ("e", 1), ("e", 2))
TRIPS = (
    (0, 1, 0, "all"),
    (0, 2, 0, "head"),
    (1, 2, 1, "head"),
    (2, 1, 2, "tail"),
    (2, 1, 3, "tail"),
    (3, 2, 3, "all"),
    (2, 3, 2, "all"),
    (2, 3, 0, "head"),
    (2, 3, 1, "head"),
    (1, 2, 0, "tail"),
    (1, 2, 1, "tail"),
    (2, 3, 0, "tail"),
    (2, 3, 1, "tail"),
)


def split_three(value):
    high = value.astype(jnp.bfloat16)
    rest = value - high.astype(jnp.float32)
    middle = rest.astype(jnp.bfloat16)
    low = (rest - middle.astype(jnp.float32)).astype(jnp.bfloat16)
    return jnp.concatenate([high, middle, low], axis=0)


def groups_of(parts, width):
    info = {}
    at = 0
    for name, blocks in GROUPS.items():
        unit = -(-(len(blocks) * width) // (parts * 8)) * 8
        info[name] = (at, unit, unit * parts, len(blocks) * width)
        at += unit * parts
    folds = {}
    deep = 0
    for number, (name, _) in enumerate(FOLDS):
        folds[number] = deep
        deep += info[name][1]
    return info, at, folds, deep


def kernel(
    parts,
    splits,
    x_any,
    mass_any,
    stiff_any,
    nodes_any,
    rigid_any,
    rows_any,
    spring_any,
    low_any,
    top_any,
    out_ref,
    x_ref,
    mass_ref,
    stiff_ref,
    nodes_ref,
    rigid_ref,
    rows_ref,
    spring_ref,
    low_ref,
    top_ref,
    value_ref,
    first_ref,
    link_ref,
    diag_ref,
    hot_ref,
    force_ref,
    send_buf,
    recv_buf,
    cols_ref,
    part_ref,
    fold_ref,
    all_ref,
    inv_ref,
    fac_ref,
    load_sem,
    ex_send,
    ex_recv,
    trip_send,
    trip_recv,
    fold_send,
    fold_recv,
    give_send,
    give_recv,
    row_send,
    row_recv,
):
    me = lax.axis_index("rows")
    col = lax.axis_index("vecs")
    count, width = x_ref.shape
    slots = rows_ref.shape[1]
    total_rows = count * parts
    unroll = parts <= 8

    barrier = pltpu.get_barrier_semaphore()
    for k in range(1, splits):
        pl.semaphore_signal(
            barrier, inc=1, device_id=(me, lax.rem(col + k, splits)), device_id_type=MESH
        )

    def greet(k, carry):
        pl.semaphore_signal(
            barrier, inc=1, device_id=(lax.rem(me + k, parts), col), device_id_type=MESH
        )
        return carry

    lax.fori_loop(1, parts, greet, 0)

    loads = [
        pltpu.make_async_copy(source, target, load_sem.at[n])
        for n, (source, target) in enumerate(
            [
                (x_any, x_ref),
                (mass_any, mass_ref),
                (stiff_any, stiff_ref),
                (nodes_any, nodes_ref),
                (rigid_any, rigid_ref),
                (rows_any, rows_ref),
                (spring_any, spring_ref),
                (low_any, low_ref),
                (top_any, top_ref),
            ]
        )
    ]
    for load in loads:
        load.start()

    chunk = count // splits
    zero_pad = jnp.zeros((PAD, width), jnp.float32)
    for ref in (value_ref, first_ref, link_ref):
        ref[0:PAD, :] = zero_pad
        ref[PAD + count :, :] = zero_pad
    force_ref[...] = jnp.zeros_like(force_ref)
    for load in loads:
        load.wait()

    top = jnp.full((1, width), top_ref[0], jnp.float32)
    bottom = jnp.full((1, width), low_ref[0], jnp.float32)
    center = (top + bottom) * 0.5
    inverse_half = 1.0 / ((top - bottom) * 0.5)

    for lo in range(0, count, chunk):
        value_ref[PAD + lo : PAD + lo + chunk, :] = x_ref[lo : lo + chunk, :].astype(jnp.float32)

    def remote(turn, k, target):
        return pltpu.make_async_remote_copy(
            src_ref=send_buf.at[turn, target],
            dst_ref=recv_buf.at[turn, me],
            send_sem=ex_send.at[turn, k],
            recv_sem=ex_recv.at[turn, k],
            device_id=(target, col),
            device_id_type=MESH,
        )

    def arrival(turn, k):
        source = lax.rem(me + parts - k, parts)
        return pltpu.make_async_remote_copy(
            src_ref=send_buf.at[turn, source],
            dst_ref=recv_buf.at[turn, source],
            send_sem=ex_send.at[turn, k],
            recv_sem=ex_recv.at[turn, k],
            device_id=(source, col),
            device_id_type=MESH,
        )

    def pick_anchors(turn, ref):
        first_row = ref[PAD + CABLE_ROWS : PAD + CABLE_ROWS + 1, :]
        last_row = ref[PAD + count - 1 : PAD + count, :]
        blank = jnp.zeros((8 - slots - 2, width), jnp.float32)

        def pick(q, carry):
            picked = [
                ref[pl.ds(PAD + jnp.minimum(rows_ref[0, s, q], count - 1), 1), :] for s in range(slots)
            ]
            send_buf[turn, q] = jnp.concatenate(picked + [first_row, last_row, blank], axis=0)
            return carry

        lax.fori_loop(0, parts, pick, 0, unroll=unroll)

    def push_anchors(turn):
        def push(k, carry):
            remote(turn, k, lax.rem(me + k, parts)).start()
            return carry

        lax.fori_loop(1, parts, push, 0, unroll=unroll)
        recv_buf[turn, me] = send_buf[turn, me]

    def collect(turn, scale):
        def take(k, carry):
            arrival(turn, k).wait_recv()
            return carry

        lax.fori_loop(1, parts, take, 0, unroll=unroll)

        def pull(q, carry):
            difference = send_buf[turn, q] - recv_buf[turn, q]
            for s in range(slots):
                live = jnp.where(rows_ref[0, s, q] < count, spring_ref[0, s, q], 0.0)
                force_ref[pl.ds(q * slots + s, 1), :] = live * difference[s : s + 1, :]
            return carry

        lax.fori_loop(0, parts, pull, 0, unroll=unroll)
        before = recv_buf[turn, lax.rem(me + parts - 1, parts)]
        after = recv_buf[turn, lax.rem(me + 1, parts)]
        own = send_buf[turn, me]
        left_open = jnp.where(me > 0, rigid_ref[0], 0.0)
        right_open = jnp.where(me < parts - 1, rigid_ref[0], 0.0)
        edge = jnp.concatenate(
            [
                left_open * (own[slots : slots + 1] - before[slots + 1 : slots + 2]),
                right_open * (own[slots + 1 : slots + 2] - after[slots : slots + 1]),
                jnp.zeros((6, width), jnp.float32),
            ],
            axis=0,
        )
        force_ref[parts * slots : parts * slots + 8, :] = edge
        return split_three(force_ref[...] * scale)

    pick_anchors(0, value_ref)

    forces = force_ref.shape[0]
    order = lax.rem(lax.broadcasted_iota(jnp.int32, (1, 3 * forces), 1), forces)
    ends = parts * slots
    target = jnp.where(order == ends, CABLE_ROWS, jnp.where(order == ends + 1, count - 1, count))

    def place_anchor(q, carry):
        for s in range(slots):
            carry = jnp.where(order == q * slots + s, rows_ref[0, s, q], carry)
        return carry

    target = lax.fori_loop(0, parts, place_anchor, target, unroll=unroll)

    lane = lax.broadcasted_iota(jnp.int32, (1, width), 1)
    rigid = rigid_ref[0]
    cuts = []
    running = nodes_ref[0, 0]
    for j in range(1, nodes_ref.shape[1]):
        cuts.append(running)
        running = running + nodes_ref[0, j]
    cuts.append(running)
    for r in range(count // width):
        place = lane + r * width
        open_link = place < CABLE_ROWS - 1
        for cut in cuts:
            open_link = open_link & (place + 1 != cut)
        deck_link = (place >= CABLE_ROWS) & (place < count - 1)
        link = jnp.where(open_link, stiff_ref[r : r + 1, :], jnp.where(deck_link, rigid, 0.0))
        lo = PAD + r * width
        link_ref[lo : lo + width, :] = jnp.broadcast_to(link, (width, width)).T
        mass = mass_ref[r : r + 1, :] - center
        diag_ref[r * width : (r + 1) * width, :] = jnp.broadcast_to(mass, (width, width)).T

    def base(ref, lo):
        at = PAD + lo
        here = ref[at : at + chunk, :]
        down = link_ref[at : at + chunk, :] * (here - ref[at + 1 : at + chunk + 1, :])
        up = link_ref[at - 1 : at + chunk - 1, :] * (here - ref[at - 1 : at + chunk - 1, :])
        return diag_ref[lo : lo + chunk, :] * here + down + up

    for lo in range(0, count, chunk):
        first_ref[PAD + lo : PAD + lo + chunk, :] = base(value_ref, lo) * inverse_half
        node = lax.broadcasted_iota(jnp.int32, (chunk, 3 * forces), 0) + lo
        hot_ref[lo : lo + chunk, :] = jnp.where(node == target, 1.0, 0.0).astype(jnp.bfloat16)

    pl.semaphore_wait(barrier, parts - 1 + splits - 1)
    push_anchors(0)
    pulls = collect(0, inverse_half)
    for lo in range(0, count, chunk):
        first_ref[PAD + lo : PAD + lo + chunk, :] += jnp.dot(
            hot_ref[lo : lo + chunk, :], pulls, preferred_element_type=jnp.float32
        )
    pick_anchors(1, first_ref)
    push_anchors(1)
    double = 2.0 * inverse_half
    for lo in range(0, count, chunk):
        diag_ref[lo : lo + chunk, :] = (
            base(first_ref, lo) * double - value_ref[PAD + lo : PAD + lo + chunk, :]
        )
    pulls = collect(1, double)

    def inner(left, right):
        return lax.dot_general(
            left, right, (((0,), (0,)), ((), ())), preferred_element_type=jnp.float32
        )

    own_gram = jnp.zeros((width, width), jnp.float32)
    for lo in range(0, count, chunk):
        made = (
            diag_ref[lo : lo + chunk, :]
            + jnp.dot(hot_ref[lo : lo + chunk, :], pulls, preferred_element_type=jnp.float32)
        ).astype(jnp.bfloat16)
        cols_ref[col, lo : lo + chunk, :] = made
        own_gram = own_gram + inner(made, made)

    info, _, folds, _ = groups_of(parts, width)
    upper = count // 3

    def trip(number):
        _, target, block, place = TRIPS[number]
        lo, size = {"all": (0, count), "head": (0, upper), "tail": (upper, count - upper)}[place]
        return pltpu.make_async_remote_copy(
            src_ref=cols_ref.at[block, pl.ds(lo, size)],
            dst_ref=cols_ref.at[block, pl.ds(lo, size)],
            send_sem=trip_send.at[number],
            recv_sem=trip_recv.at[number],
            device_id=(me, target),
            device_id_type=MESH,
        )

    def fold(number, source, target, k):
        name, _ = FOLDS[number]
        at, unit, _, _ = info[name]
        return pltpu.make_async_remote_copy(
            src_ref=part_ref.at[pl.ds(pl.multiple_of(at + target * unit, 8), unit)],
            dst_ref=fold_ref.at[source, pl.ds(folds[number], unit)],
            send_sem=fold_send.at[number, k],
            recv_sem=fold_recv.at[number, k],
            device_id=(target, OWNER[name]),
            device_id_type=MESH,
        )

    def skip(number):
        name, source = FOLDS[number]
        return 1 if source == OWNER[name] else 0

    def fold_start(number):
        def act(k, carry):
            fold(number, me, lax.rem(me + k, parts), k).start()
            return carry

        lax.fori_loop(skip(number), parts, act, 0, unroll=unroll)

    def fold_end(number):
        def act(k, carry):
            fold(number, me, lax.rem(me + k, parts), k).wait_send()
            return carry

        lax.fori_loop(skip(number), parts, act, 0, unroll=unroll)

    def place_of(name, owner):
        at, unit, _, _ = info[name]
        return pl.ds(pl.multiple_of(at + owner * unit, 8), unit)

    def fold_sum(name, numbers):
        _, unit, _, _ = info[name]
        total = jnp.zeros((unit, width), jnp.float32)
        for number in numbers:
            if skip(number):
                total = total + part_ref[place_of(name, me), :]

            def act(k, carry):
                source = lax.rem(me + parts - k, parts)
                fold(number, source, me, k).wait_recv()
                return carry + fold_ref[source, folds[number] : folds[number] + unit, :]

            total = lax.fori_loop(skip(number), parts, act, total, unroll=unroll)
        all_ref[place_of(name, me), :] = total

    def give(name, owner, target, k):
        n = list(GROUPS).index(name)
        return pltpu.make_async_remote_copy(
            src_ref=all_ref.at[place_of(name, owner)],
            dst_ref=all_ref.at[place_of(name, owner)],
            send_sem=give_send.at[n, k],
            recv_sem=give_recv.at[n, k],
            device_id=(target, splits - 1),
            device_id_type=MESH,
        )

    def give_skip(name):
        return 1 if OWNER[name] == splits - 1 else 0

    def give_start(name):
        def act(k, carry):
            give(name, me, lax.rem(me + k, parts), k).start()
            return carry

        lax.fori_loop(give_skip(name), parts, act, 0, unroll=unroll)

    def give_end(name):
        def act(k, carry):
            give(name, me, lax.rem(me + k, parts), k).wait_send()
            return carry

        lax.fori_loop(give_skip(name), parts, act, 0, unroll=unroll)

    def give_take(name):
        def act(k, carry):
            give(name, lax.rem(me + parts - k, parts), me, k).wait_recv()
            return carry

        lax.fori_loop(give_skip(name), parts, act, 0, unroll=unroll)

    def store_part(name, blocks):
        at, _, length, used = info[name]
        for n, block in enumerate(blocks):
            part_ref[at + n * width : at + (n + 1) * width, :] = block
        if used < length:
            part_ref[at + used : at + length, :] = jnp.zeros((length - used, width), jnp.float32)

    def factor_row(k):
        return pltpu.make_async_remote_copy(
            src_ref=fac_ref.at[k, :, pl.ds(0, (k + 1) * width)],
            dst_ref=fac_ref.at[k, :, pl.ds(0, (k + 1) * width)],
            send_sem=row_send.at[k],
            recv_sem=row_recv.at[k],
            device_id=(me, k),
            device_id_type=MESH,
        )

    def finish(device):
        used_width = (device + 1) * width
        factor = fac_ref[device, :, :used_width]
        for lo in range(0, count, chunk):
            block = jnp.concatenate(
                [cols_ref[b, lo : lo + chunk, :] for b in range(device + 1)], axis=1
            )
            out_ref[lo : lo + chunk, :] = lax.dot_general(
                block, factor, (((1,), (1,)), ((), ())), preferred_element_type=jnp.float32
            ).astype(jnp.bfloat16)

    def close(trips, numbers, names):
        for n in trips:
            trip(n).wait_send()
        for number in numbers:
            fold_end(number)
        for name in names:
            give_end(name)

    @pl.when(col == 0)
    def _():
        trip(0).start()
        store_part("a", [own_gram])
        fold_start(0)
        trip(1).start()
        factor_row(0).wait_recv()
        finish(0)
        close([0, 1], [0], [])

    @pl.when(col == 1)
    def _():
        trip(0).wait_recv()
        cross = jnp.zeros((width, width), jnp.float32)
        for lo in range(0, count, chunk):
            cross = cross + inner(cols_ref[1, lo : lo + chunk, :], cols_ref[0, lo : lo + chunk, :])
        store_part("b", [cross, own_gram])
        fold_start(1)
        trip(2).start()
        for number, block, name, fold_number, later in ((3, 2, "c", 3, 9), (4, 3, "e", 5, 10)):
            trip(number).wait_recv()
            cross = jnp.zeros((width, 2 * width), jnp.float32)
            for lo in range(upper, count, upper):
                cross = cross + inner(
                    cols_ref[block, lo : lo + upper, :],
                    jnp.concatenate(
                        [cols_ref[0, lo : lo + upper, :], cols_ref[1, lo : lo + upper, :]], axis=1
                    ),
                )
            store_part(name, [cross[:, :width], cross[:, width:]])
            fold_start(fold_number)
            trip(later).start()
        factor_row(1).wait_recv()
        finish(1)
        close([2, 9, 10], [1, 3, 5], [])

    @pl.when(col == 2)
    def _():
        trip(3).start()
        trip(6).start()
        trip(5).wait_recv()
        trip(4).start()
        cross = jnp.zeros((width, 2 * width), jnp.float32)
        for lo in range(0, count, chunk):
            third = cols_ref[3, lo : lo + chunk, :]
            cross = cross + inner(
                third, jnp.concatenate([cols_ref[2, lo : lo + chunk, :], third], axis=1)
            )
        store_part("d", [own_gram, cross[:, :width], cross[:, width:]])
        fold_start(2)
        fold_sum("b", [1])
        give_start("b")
        fold_sum("d", [2])
        give_start("d")
        trip(1).wait_recv()
        trip(2).wait_recv()
        pair = jnp.concatenate([cols_ref[0, :upper, :], cols_ref[1, :upper, :]], axis=1)
        cross = inner(jnp.concatenate([cols_ref[2, :upper, :], cols_ref[3, :upper, :]], axis=1), pair)
        store_part("c", [cross[:width, :width], cross[:width, width:]])
        fold_start(4)
        store_part("e", [cross[width:, :width], cross[width:, width:]])
        fold_start(6)
        trip(7).start()
        trip(8).start()
        fold_sum("c", [4, 3])
        give_start("c")
        fold_sum("e", [6, 5])
        give_start("e")
        trip(9).wait_recv()
        trip(11).start()
        trip(10).wait_recv()
        trip(12).start()
        factor_row(2).wait_recv()
        finish(2)
        close([3, 4, 6, 7, 8, 11, 12], [2, 4, 6], ["b", "c", "d", "e"])

    @pl.when(col == 3)
    def _():
        trip(5).start()
        inv_ref[...] = jnp.zeros_like(inv_ref)
        fold_sum("a", [0])
        give_start("a")
        blocks = {}
        for name, members in GROUPS.items():
            at = info[name][0]
            for n, member in enumerate(members):
                blocks[member] = at + n * width
        scale = 1.0 / total_rows

        def gram(i, j):
            at = blocks[i, j]
            return all_ref[at : at + width, :] * scale

        for k, names in enumerate(("a", "b", "dc", "e")):
            for name in names:
                give_take(name)
            lo, hi = k * width, (k + 1) * width
            rest = gram(k, k)
            if k:
                known = inv_ref[:lo, :lo]
                panel = mm(jnp.concatenate([gram(k, j) for j in range(k)], axis=1), known, ((1,), (1,)))
                rest = rest - mm(panel, panel, ((1,), (1,)))
                carried = mm(panel, known, ((1,), (0,)))
            corner = eliminate(rest)
            if k:
                side = -mm(corner, carried, ((1,), (0,)))
                inv_ref[lo:hi, :lo] = side
                fac_ref[k, :, :lo] = side.astype(jnp.bfloat16)
            inv_ref[lo:hi, lo:hi] = corner
            fac_ref[k, :, lo:hi] = corner.astype(jnp.bfloat16)
            if k < splits - 1:
                factor_row(k).start()
        for n in (6, 7, 8, 11, 12):
            trip(n).wait_recv()
        finish(splits - 1)
        close([5], [], ["a"])
        for k in range(splits - 1):
            factor_row(k).wait_send()

    def settle(k, carry):
        target = lax.rem(me + k, parts)
        remote(0, k, target).wait_send()
        remote(1, k, target).wait_send()
        return carry

    lax.fori_loop(1, parts, settle, 0, unroll=unroll)


def body(
    parts,
    splits,
    vectors,
    node_mass,
    cable_stiff,
    cable_nodes,
    deck_rigidity,
    anchor_rows,
    anchor_stiff,
    cut_low,
    top_bound,
):
    count, width = vectors.shape
    slots = anchor_rows.shape[2]
    forces = parts * slots + 8
    size = splits * width
    _, length, _, deep = groups_of(parts, width)
    sem = pltpu.SemaphoreType.DMA
    f32 = jnp.float32
    args = (
        vectors,
        node_mass.reshape(-1, width),
        cable_stiff.reshape(-1, width),
        cable_nodes,
        deck_rigidity.reshape(1),
        jnp.transpose(anchor_rows, (0, 2, 1)),
        jnp.transpose(anchor_stiff, (0, 2, 1)),
        cut_low.reshape(1),
        top_bound.reshape(1),
    )
    return pl.pallas_call(
        functools.partial(kernel, parts, splits),
        out_shape=jax.ShapeDtypeStruct((count, width), jnp.bfloat16),
        in_specs=[pl.BlockSpec(memory_space=pl.ANY)] * len(args),
        out_specs=pl.BlockSpec(memory_space=pltpu.VMEM),
        scratch_shapes=[pltpu.VMEM(a.shape, a.dtype) for a in args[:3]]
        + [pltpu.SMEM(a.shape, a.dtype) for a in args[3:]]
        + [
            pltpu.VMEM((count + 2 * PAD, width), f32),
            pltpu.VMEM((count + 2 * PAD, width), f32),
            pltpu.VMEM((count + 2 * PAD, width), f32),
            pltpu.VMEM((count, width), f32),
            pltpu.VMEM((count, 3 * forces), jnp.bfloat16),
            pltpu.VMEM((forces, width), f32),
            pltpu.VMEM((2, parts, 8, width), f32),
            pltpu.VMEM((2, parts, 8, width), f32),
            pltpu.VMEM((splits, count, width), jnp.bfloat16),
            pltpu.VMEM((length, width), f32),
            pltpu.VMEM((parts, deep, width), f32),
            pltpu.VMEM((length, width), f32),
            pltpu.VMEM((size, size), f32),
            pltpu.VMEM((splits, width, size), jnp.bfloat16),
            sem((len(args),)),
            sem((2, parts)),
            sem((2, parts)),
            sem((len(TRIPS),)),
            sem((len(TRIPS),)),
            sem((len(FOLDS), parts)),
            sem((len(FOLDS), parts)),
            sem((len(GROUPS), parts)),
            sem((len(GROUPS), parts)),
            sem((splits - 1,)),
            sem((splits - 1,)),
        ],
        compiler_params=pltpu.CompilerParams(
            collective_id=0, has_side_effects=True, vmem_limit_bytes=60 * 1024 * 1024
        ),
    )(*args)


def solution(mesh):
    return jax.shard_map(
        functools.partial(body, mesh.shape["rows"], mesh.shape["vecs"]),
        mesh=mesh,
        in_specs=(
            P("rows", "vecs"),
            P("rows"),
            P("rows"),
            P("rows", None),
            P(),
            P("rows", None, None),
            P("rows", None, None),
            P(),
            P(),
        ),
        out_specs=P("rows", "vecs"),
        check_vma=False,
    )
```

time: 73.7 us -> 52 us (0.71)
  Pallas kernels: 67.4 us -> 47.8 us
  local copies, waits for them, and re-layouts: 4.09 us -> 2.06 us
    pallas_call x1, Pallas kernels: 67.4 us -> 47.8 us  [body(): pl.pallas_call(functools.partial(kernel, parts, splits), out_shape=jax.Sh...]
    unnamed x7 -> x1, local copies, waits for them, and re-layouts: 4.09 us -> 2.06 us
where the time goes in v1:
time: 52 us; the launch traced here: 51.8 us
  Pallas kernels  47.8 us (92%)
  local copies, waits for them, and re-layouts  2.06 us (4%)
  between operations  1.95 us (4%)
    pallas_call x1, Pallas kernels, body(): pl.pallas_call(functools.partial(kernel, parts, splits), out_shape=jax.Sh...  47.8 us
    unnamed x1, local copies, waits for them, and re-layouts  2.06 us

profile of v1, /device:TPU:3, one launch (start us, length us, event | category | flops | bytes accessed | tf_op | source)
XLA Modules:
  0.0 51.8 jit_solution(2883909045279943762)
XLA Ops:
  1.9 47.8 %shard_map.91 = bf16[3072,128]{1,0:T(8,128)(2,1)} custom-call(bf16[3072,128]{1,0:T(8,128)(2,1)} %x_any.1, f32[24,128]{1,0:T(8,128)} %bitcast.10, f32[24,128]{1,0:T(8,128)} %bitcast.11, s32[1,4]{1,0:T(1,128)} %nodes_any.1, f32[1]{0:T(128)} %bitcast.7.rigid_any, s32[1,4,8]{2,1,0:T(4,128)} %bitcast.12, f32[1,4,8]{2,1,0:T(4,128)} %bitcast.13, f32[1]{0:T(128)} %bitcast.8.low_any, ...), custom_call_target="tpu_custom_call" | custom-call | tf_op jit(solution)/shard_map/pallas_call | solution.py:660
  49.8 2.1 %copy.14 = bf16[3072,128]{1,0:T(8,128)(2,1)} copy(bf16[3072,128]{1,0:T(8,128)(2,1)} %shard_map.91) | data formatting | bytes 1572864
